TPU v7x, 32 devices: a whole 2x2x4 slice. The times are simulated.
32 devices in a mesh: layer: 4 (over y, core), latent: 8 (over z, x).
Axes of the slice: x: 2, y: 2, z: 4, core: 2. Of those that a mesh axis runs over, the one named last changes fastest.
Arguments:
- inputs: bfloat16 [4, 128, 4096], P('layer', 'latent'), may hold values from -6 to 6
- targets: bfloat16 [4, 128, 4096], P('layer', 'latent'), may hold values from -6 to 6
- w_enc: bfloat16 [4, 4096, 8192], P('layer', None, 'latent'), may hold values from -0.09375 to 0.09375
- b_enc: float32 [4, 8192], P('layer', 'latent'), may hold values from -3 to 3
- w_dec: bfloat16 [4, 4, 8192, 4096], P('layer', None, 'latent'), may hold values from -0.03125 to 0.03125
- b_dec: float32 [4, 4096], P('layer'), may hold values from -3 to 3
Outputs:
- grad_enc: bfloat16 [4, 4096, 8192], P('layer', None, 'latent')
- grad_benc: float32 [4, 8192], P('layer', 'latent')
- grad_dec: bfloat16 [4, 4, 8192, 4096], P('layer', None, 'latent')
- grad_bdec: float32 [4, 4096], P('layer')
All inputs are finite; a program needn't handle non-finite values.
Results may differ from a plain program's by a relative error of at most 0.0057.
Values may be sent and summed in bfloat16 or wider, within the bound.
A program may use at most 192 MiB of HBM per device.

v0:
```python
import jax
import jax.numpy as jnp
from jax import lax
from jax.sharding import PartitionSpec as P

penalty = 0.5
eps = 1e-06


def local(inputs, targets, w_enc, b_enc, w_dec, b_dec):
    source = lax.axis_index("layer")
    depth = w_dec.shape[1]
    whole = lax.all_gather(inputs[0], "latent", axis=0, tiled=True)
    pre = jnp.dot(whole, w_enc[0], preferred_element_type=jnp.float32) + b_enc[0]
    positive = jnp.maximum(pre, 0.0)
    act = (positive * positive).astype(jnp.bfloat16)
    valid = (jnp.arange(depth, dtype=jnp.int32) >= source).astype(jnp.float32)
    partial_value = (
        jnp.einsum("nk,tkd->tnd", act, w_dec[0], preferred_element_type=jnp.float32)
        * valid[:, None, None]
    )
    spread = lax.psum_scatter(partial_value, "layer", scatter_dimension=0, tiled=True)
    recon = lax.psum_scatter(spread, "latent", scatter_dimension=1, tiled=True)
    error = recon[0] + b_dec[0] - targets[0].astype(jnp.float32)
    grad_bdec = lax.psum(jnp.sum(error, axis=0), "latent")[None, :]
    err_low = error.astype(jnp.bfloat16)[None]
    stacked = lax.all_gather(err_low, "latent", axis=1, tiled=True)
    errors = lax.all_gather(stacked, "layer", axis=0, tiled=True)
    errors = jnp.where(valid[:, None, None] > 0.0, errors, jnp.zeros_like(errors))
    decoders = w_dec[0]
    squares = jnp.sum(jnp.square(decoders.astype(jnp.float32)), axis=2)
    norms = jnp.sqrt(jnp.sum(squares * valid[:, None], axis=0) + eps)
    back = jnp.einsum("tnd,tkd->nk", errors, decoders, preferred_element_type=jnp.float32)
    d_act = back + penalty * norms[None, :]
    d_pre = d_act * 2.0 * positive
    grad_benc = jnp.sum(d_pre, axis=0)[None, :]
    d_low = d_pre.astype(jnp.bfloat16)
    grad_enc = lax.dot_general(
        whole, d_low, (((0,), (0,)), ((), ())), preferred_element_type=jnp.float32
    ).astype(jnp.bfloat16)[None]
    act_total = jnp.sum(act.astype(jnp.float32), axis=0)
    scale = penalty * act_total / norms
    grad_mse = jnp.einsum("nk,tnd->tkd", act, errors, preferred_element_type=jnp.float32)
    shrink = valid[:, None, None] * scale[None, :, None] * decoders.astype(jnp.float32)
    grad_dec = (grad_mse + shrink).astype(jnp.bfloat16)[None]
    return (grad_enc, grad_benc, grad_dec, grad_bdec)


def solution(mesh):
    placed = (
        P("layer", "latent", None),
        P("layer", "latent", None),
        P("layer", None, "latent"),
        P("layer", "latent"),
        P("layer", None, "latent", None),
        P("layer", None),
    )
    return jax.shard_map(
        local,
        mesh=mesh,
        in_specs=placed,
        out_specs=(
            P("layer", None, "latent"),
            P("layer", "latent"),
            P("layer", None, "latent", None),
            P("layer", None),
        ),
        check_vma=False,
    )
```

profile of v0, /device:TPU:0, one launch (start us, length us, event | category | flops | bytes accessed | tf_op | source)
XLA Modules:
  0.0 456.9 jit_solution(2697420618974324879)
XLA Ops:
  7.2 0.0 all-gather.9.cloned.1.call-start
  7.2 0.7 all-gather.9.cloned.1.call-update
  7.9 0.0 reduce-scatter.3.cloned.1.call-start
  8.0 45.2 %all-gather.9.cloned.1.call-done = bf16[1,128,4096]{2,1,0:T(8,128)(2,1)} async-done(((bf16[1,16,4096]{2,1,0:T(8,128)(2,1)}), bf16[1,128,4096]{2,1,0:T(8,128)(2,1)}) %all-gather.9.cloned.1.call-update) | async-done | bytes 1048592 | tf_op jit(solution)/shard_map/all_gather | solution.py:13
  53.1 4.9 %convert_reduce_fusion = (f32[1024]{0:T(1024)S(1)}, f32[128,1024]{1,0:T(8,128)S(1)}) fusion(f32[1024]{0:T(1024)} %bitcast.82, bf16[1,4096,1024]{2,1,0:T(8,128)(2,1)} %param.8, bf16[1,128,4096]{2,1,0:T(8,128)(2,1)} %all-gather.9.cloned.1.call-done), kind=kOutput, calls=%fused_computation.23 | convolution fusion | flops 1074527232 | bytes 9969664 | tf_op jit(solution)/shard_map/dot_general | solution.py:14
  58.0 18.5 %multiply_bitcast_fusion = f32[4,128,4096]{2,1,0:T(8,128)} fusion(f32[4]{0:T(128)S(1)} %compare_convert_fusion, bf16[1,4,1024,4096]{3,2,1,0:T(8,128)(2,1)} %param.10, f32[128,1024]{1,0:T(8,128)S(1)} %get-tuple-element.15), kind=kOutput, calls=%fused_computation.13 | convolution fusion | flops 4297326592 | bytes 42467344 | tf_op jit(solution)/shard_map/nk,tkd->tnd/dot_general | solution.py:19
  76.5 0.0 copy-start.2
  76.5 0.0 copy-start.3
  76.5 0.0 reduce-scatter.3.cloned.1.call-update
  76.6 0.0 reduce-scatter.5.cloned.1.call-start
  76.6 70.2 %reduce-scatter.3.cloned.1.call-done = f32[1,128,4096]{2,1,0:T(8,128)} async-done(((f32[4,128,4096]{2,1,0:T(8,128)}), f32[1,128,4096]{2,1,0:T(8,128)}) %reduce-scatter.3.cloned.1.call-update) | async-done | bytes 2097168 | tf_op jit(solution)/shard_map/reduce_scatter | solution.py:22
  146.9 0.0 reduce-scatter.5.cloned.1.call-update
  146.9 0.0 all-gather.5.cloned.1.call-start
  146.9 72.2 %reduce-scatter.5.cloned.1.call-done = f32[1,16,4096]{2,1,0:T(8,128)} async-done(((f32[1,128,4096]{2,1,0:T(8,128)}), f32[1,16,4096]{2,1,0:T(8,128)}) %reduce-scatter.5.cloned.1.call-update) | async-done | bytes 262160 | tf_op jit(solution)/shard_map/reduce_scatter | solution.py:23
  219.2 0.0 copy-done.2
  219.2 0.0 copy-done.3
  219.2 1.6 fusion.32
  220.8 0.0 all-gather.5.cloned.1.call-update
  220.8 0.0 all-gather.7.cloned.1.call-start
  220.9 40.2 %all-gather.5.cloned.1.call-done = bf16[1,128,4096]{2,1,0:T(8,128)(2,1)} async-done(((bf16[1,16,4096]{2,1,0:T(8,128)(2,1)}), bf16[1,128,4096]{2,1,0:T(8,128)(2,1)}) %all-gather.5.cloned.1.call-update) | async-done | bytes 1048592 | tf_op jit(solution)/shard_map/all_gather | solution.py:27
  261.1 0.0 all-gather.7.cloned.1.call-update
  261.1 40.6 %copy.16 = bf16[1,4,1024,4096]{2,3,1,0:T(8,128)(2,1)} copy(bf16[1,4,1024,4096]{3,2,1,0:T(8,128)(2,1)} %param.10) | data formatting | bytes 67108864 | tf_op args[4]
  301.6 0.0 copy-start.1
  301.7 11.7 %fusion = f32[4,1024]{1,0:T(4,128)S(1)} fusion(bf16[1,4,1024,4096]{2,3,1,0:T(8,128)(2,1)} %copy.16), kind=kLoop, calls=%fused_computation.2 | loop fusion | flops 50327552 | bytes 33570816 | tf_op jit(solution)/shard_map/reduce_sum | solution.py:31
  313.4 0.1 multiply_reduce_fusion
  313.5 0.1 broadcast_multiply_fusion
  313.5 0.0 copy-done.1
  313.5 0.1 fusion.34
  313.6 35.7 %psum.7 = f32[1,4096]{1,0:T(1,128)} all-reduce(f32[1,4096]{1,0:T(1,128)S(1)} %bitcast.81), channel_id=1, replica_groups=mesh['layer'=4,'latent'=8] {'latent'}, use_global_device_ids=true, to_apply=%region_7.8 | all-reduce | flops 4096 | bytes 32768 | tf_op jit(solution)/shard_map/psum | solution.py:25
  349.3 0.0 all-gather.7.cloned.1.call-done
  349.3 25.4 %fusion.7 = bf16[1,4,1024,4096]{2,3,1,0:T(8,128)(2,1)} fusion(bf16[1,4,1024,4096]{2,3,1,0:T(8,128)(2,1)} %copy.16, f32[4,1024]{1,0:T(4,128)S(1)} %broadcast_multiply_fusion, bf16[4,128,4096]{2,1,0:T(8,128)(2,1)} %all-gather.7.cloned.1.call-done, pred[4]{0:T(512)(128)(4,1)S(1)} %broadcast_compare_fusion, f32[128,1024]{1,0:T(8,128)S(1)} %get-tuple-element.15), kind=kOutput, calls=%fused_computation.9 | convolution fusion | flops 4364435456 | bytes 71843840 | tf_op jit(solution)/shard_map/nk,tnd->tkd/dot_general | solution.py:43
  374.7 40.5 %copy.21 = bf16[1,4,1024,4096]{3,2,1,0:T(8,128)(2,1)} copy(bf16[1,4,1024,4096]{2,3,1,0:T(8,128)(2,1)} %fusion.7) | data formatting | bytes 67108864
  415.2 0.0 copy-start
  415.2 17.6 %fusion.40 = (f32[1024]{0:T(1024)}, bf16[128,1024]{1,0:T(8,128)(2,1)S(1)}) fusion(f32[128,1024]{1,0:T(8,128)S(1)} %get-tuple-element.15, f32[1024]{0:T(1024)S(1)} %get-tuple-element.13, bf16[1,4,1024,4096]{3,2,1,0:T(8,128)(2,1)} %param.10, bf16[4,128,4096]{2,1,0:T(8,128)(2,1)} %all-gather.7.cloned.1.call-done, pred[4]{0:T(512)(128)(4,1)S(1)} %broadcast_compare_fusion), kind=kOutput, calls=%fused_computation.42 | convolution fusion | flops 4297718784 | bytes 38543364 | tf_op jit(solution)/shard_map/tnd,tkd->nk/dot_general | solution.py:33
  432.8 0.0 copy-done
  432.8 5.6 %convert_bitcast_fusion = bf16[1,4096,1024]{1,2,0:T(8,128)(2,1)} fusion(bf16[1,128,4096]{2,1,0:T(8,128)(2,1)S(1)} %copy-done, bf16[128,1024]{1,0:T(8,128)(2,1)S(1)} %get-tuple-element.17), kind=kOutput, calls=%fused_computation.12 | convolution fusion | flops 1077936128 | bytes 9699328 | tf_op jit(solution)/shard_map/dot_general | solution.py:38
  438.4 11.9 %copy.20 = bf16[1,4096,1024]{2,1,0:T(8,128)(2,1)} copy(bf16[1,4096,1024]{1,2,0:T(8,128)(2,1)} %convert_bitcast_fusion) | data formatting | bytes 16777216
  (3 shorter events, 0.0 us)
Async XLA Ops:
  7.2 46.0 %all-gather.9.cloned.1.call-start = ((), (), s32[]{:S(2)}) async-start(), calls=%async_computation.6 | async-start | bytes 1179648 | tf_op jit(solution)/shard_map/all_gather | solution.py:13
  7.9 139.0 %reduce-scatter.3.cloned.1.call-start = ((), (), s32[]{:S(2)}) async-start(), calls=%async_computation.2 | async-start | bytes 10485760 | tf_op jit(solution)/shard_map/reduce_scatter | solution.py:22
  76.5 142.6 %copy-start.2 = (bf16[1,16,4096]{2,1,0:T(8,128)(2,1)S(1)}, bf16[1,16,4096]{2,1,0:T(8,128)(2,1)}, u32[]{:S(2)}) copy-start(bf16[1,16,4096]{2,1,0:T(8,128)(2,1)} %param.7) | copy-start | bytes 393220
  76.5 142.6 %copy-start.3 = (f32[1,4096]{1,0:T(1,128)S(1)}, f32[1,4096]{1,0:T(1,128)}, u32[]{:S(2)}) copy-start(f32[1,4096]{1,0:T(1,128)} %param.11) | copy-start | bytes 49156
  76.6 142.6 %reduce-scatter.5.cloned.1.call-start = ((), (), s32[]{:S(2)}) async-start(), calls=%async_computation.3 | async-start | bytes 2359296 | tf_op jit(solution)/shard_map/reduce_scatter | solution.py:23
  146.9 114.2 %all-gather.5.cloned.1.call-start = ((), (), s32[]{:S(2)}) async-start(), calls=%async_computation.4 | async-start | bytes 1179648 | tf_op jit(solution)/shard_map/all_gather | solution.py:27
  220.8 128.5 %all-gather.7.cloned.1.call-start = ((), (), s32[]{:S(2)}) async-start(), calls=%async_computation.5 | async-start | bytes 5242880 | tf_op jit(solution)/shard_map/all_gather | solution.py:28
  301.6 11.9 %copy-start.1 = (f32[1,16,4096]{2,1,0:T(8,128)S(1)}, f32[1,16,4096]{2,1,0:T(8,128)}, u32[]{:S(2)}) copy-start(f32[1,16,4096]{2,1,0:T(8,128)} %reduce-scatter.5.cloned.1.call-done) | copy-start | bytes 786436
  415.2 17.6 %copy-start = (bf16[1,128,4096]{2,1,0:T(8,128)(2,1)S(1)}, bf16[1,128,4096]{2,1,0:T(8,128)(2,1)}, u32[]{:S(2)}) copy-start(bf16[1,128,4096]{2,1,0:T(8,128)(2,1)} %all-gather.9.cloned.1.call-done) | copy-start | bytes 3145732
Sparse Core Ops, SparseCore 0:
  10.1 42.9 all-gather.8
  76.7 70.1 reduce-scatter.2
  150.4 68.7 reduce-scatter.4
  221.7 39.2 all-gather.4
  262.5 33.1 all-gather.6
where the time goes:
time: 459 us; the launch traced here: 457 us
  waiting for transfers between devices  229 us (50%)
  local copies, waits for them, and re-layouts  93 us (20%)
  matrix products  72 us (16%)
  blocking collectives  35.7 us (8%)
  between operations  13.8 us (3%)
  other arithmetic  13.6 us (3%)
    unnamed x11, local copies, waits for them, and re-layouts  93 us
    reduce_scatter x1, waiting for transfers between devices, local(): recon = lax.psum_scatter(spread, 'latent', scatter_dimension=1, tiled=True)  72.2 us
    reduce_scatter x1, waiting for transfers between devices, local(): lax.psum_scatter(partial_value, 'layer', scatter_dimension=0, tiled=True)  70.2 us
    all_gather x1, waiting for transfers between devices, local(): whole = lax.all_gather(inputs[0], 'latent', axis=0, tiled=True)  45.2 us
    all_gather x1, waiting for transfers between devices, local(): stacked = lax.all_gather(err_low, 'latent', axis=1, tiled=True)  40.2 us
    psum x1, blocking collectives, local(): grad_bdec = lax.psum(jnp.sum(error, axis=0), 'latent')[None, :]  35.7 us
    dot_general x1, matrix products, local(): jnp.einsum('nk,tnd->tkd', act, errors, preferred_element_type=jnp.float32)  25.4 us
    dot_general x1, matrix products, local(): jnp.einsum('nk,tkd->tnd', act, w_dec[0], preferred_element_type=jnp.float32)  18.5 us
  transfers between devices with their start and end apart: 5, of which 4 were waited for; matrix products, arithmetic and copies ran while one was open for 11% of the time, Pallas kernels for 0%

commit v1 on v0

v1 whole, which is shorter than its diff:
```python
import functools

import jax
import jax.numpy as jnp
from jax import lax
from jax.experimental import pallas as pl
from jax.experimental.pallas import tpu as pltpu
from jax.sharding import PartitionSpec as P

penalty = 0.5
eps = 1e-06
f32 = jnp.float32
bf16 = jnp.bfloat16
VMEM_LIMIT = 60 * 1024 * 1024


def forward_kernel(src, whole, w_enc, b_enc, w_dec, positive, act, partial, total):
    step = pl.program_id(0)
    depth = w_dec.shape[0]
    features = w_dec.shape[2]
    cols = min(features, 1024)

    @pl.when(step == 0)
    def _():
        total[...] = jnp.zeros_like(total)

    pre = jnp.dot(whole[...], w_enc[...], preferred_element_type=f32) + b_enc[...]
    pos = jnp.maximum(pre, 0.0)
    positive[...] = pos
    act[...] = (pos * pos).astype(bf16)
    for t in range(depth):

        @pl.when(t >= src[0])
        def _():
            for c in range(0, features, cols):
                total[t, :, c : c + cols] += jnp.dot(
                    act[...], w_dec[t, :, c : c + cols], preferred_element_type=f32
                )

    @pl.when(step == pl.num_programs(0) - 1)
    def _():
        for t in range(depth):
            partial[t] = total[t].astype(partial.dtype)


def forward(src, whole, w_enc, b_enc, w_dec, out_dtype):
    tokens, features = whole.shape
    depth, latents, _ = w_dec.shape
    block = min(latents, 256)
    return pl.pallas_call(
        forward_kernel,
        grid_spec=pltpu.PrefetchScalarGridSpec(
            num_scalar_prefetch=1,
            grid=(latents // block,),
            in_specs=[
                pl.BlockSpec((tokens, features), lambda i, s: (0, 0), pipeline_mode=pl.Buffered(1)),
                pl.BlockSpec((features, block), lambda i, s: (0, i)),
                pl.BlockSpec((1, block), lambda i, s: (0, i)),
                pl.BlockSpec((depth, block, features), lambda i, s: (0, i, 0)),
            ],
            out_specs=[
                pl.BlockSpec((tokens, block), lambda i, s: (0, i)),
                pl.BlockSpec((tokens, block), lambda i, s: (0, i)),
                pl.BlockSpec((depth, tokens, features), lambda i, s: (0, 0, 0), pipeline_mode=pl.Buffered(1)),
            ],
            scratch_shapes=[pltpu.VMEM((depth, tokens, features), f32)],
        ),
        out_shape=[
            jax.ShapeDtypeStruct((tokens, latents), f32),
            jax.ShapeDtypeStruct((tokens, latents), bf16),
            jax.ShapeDtypeStruct((depth, tokens, features), out_dtype),
        ],
        compiler_params=pltpu.CompilerParams(
            dimension_semantics=("arbitrary",), vmem_limit_bytes=VMEM_LIMIT
        ),
    )(src, whole, w_enc, b_enc, w_dec)


def backward_kernel(
    src, whole, positive, act, errors, w_dec, grad_enc, grad_benc, grad_dec, flipped, back, squares
):
    depth, block, features = w_dec.shape
    cols = min(features, 512)
    lanes = 128

    @pl.when(pl.program_id(0) == 0)
    def _():
        flipped[...] = whole[...].T

    back[...] = jnp.zeros_like(back)
    squares[...] = jnp.zeros_like(squares)
    for t in range(depth):

        @pl.when(t >= src[0])
        def _():
            back[...] += lax.dot_general(
                errors[t], w_dec[t], (((1,), (1,)), ((), ())), preferred_element_type=f32
            )
            partial = squares[...]
            for c in range(0, features, lanes):
                wide = w_dec[t, :, c : c + lanes].astype(f32)
                partial = partial + wide * wide
            squares[...] = partial

    sums = squares[...]
    norm_row = jnp.sqrt(jnp.sum(sums.T, axis=0, keepdims=True) + eps)
    norm_col = jnp.sqrt(jnp.sum(sums, axis=1, keepdims=True) + eps)
    d_pre = (back[...] + penalty * norm_row) * 2.0 * positive[...]
    grad_benc[...] = jnp.sum(d_pre, axis=0, keepdims=True)
    grad_enc[...] = jnp.dot(
        flipped[...], d_pre.astype(bf16), preferred_element_type=f32
    ).astype(bf16)
    turned = act[...].astype(f32).T
    scale = penalty * jnp.sum(turned, axis=1, keepdims=True) / norm_col
    turned = turned.astype(bf16)
    for t in range(depth):

        @pl.when(t >= src[0])
        def _():
            for c in range(0, features, cols):
                mse = jnp.dot(turned, errors[t, :, c : c + cols], preferred_element_type=f32)
                grad_dec[t, :, c : c + cols] = (
                    mse + scale * w_dec[t, :, c : c + cols].astype(f32)
                ).astype(bf16)

        @pl.when(t < src[0])
        def _():
            grad_dec[t] = jnp.zeros_like(grad_dec[t])


def backward(src, whole, positive, act, errors, w_dec):
    tokens, features = whole.shape
    depth, latents, _ = w_dec.shape
    block = min(latents, 128)
    return pl.pallas_call(
        backward_kernel,
        grid_spec=pltpu.PrefetchScalarGridSpec(
            num_scalar_prefetch=1,
            grid=(latents // block,),
            in_specs=[
                pl.BlockSpec((tokens, features), lambda i, s: (0, 0), pipeline_mode=pl.Buffered(1)),
                pl.BlockSpec((tokens, block), lambda i, s: (0, i)),
                pl.BlockSpec((tokens, block), lambda i, s: (0, i)),
                pl.BlockSpec((depth, tokens, features), lambda i, s: (0, 0, 0), pipeline_mode=pl.Buffered(1)),
                pl.BlockSpec((depth, block, features), lambda i, s: (0, i, 0)),
            ],
            out_specs=[
                pl.BlockSpec((features, block), lambda i, s: (0, i)),
                pl.BlockSpec((1, block), lambda i, s: (0, i)),
                pl.BlockSpec((depth, block, features), lambda i, s: (0, i, 0)),
            ],
            scratch_shapes=[
                pltpu.VMEM((features, tokens), bf16),
                pltpu.VMEM((tokens, block), f32),
                pltpu.VMEM((block, 128), f32),
            ],
        ),
        out_shape=[
            jax.ShapeDtypeStruct((features, latents), bf16),
            jax.ShapeDtypeStruct((1, latents), f32),
            jax.ShapeDtypeStruct((depth, latents, features), bf16),
        ],
        compiler_params=pltpu.CompilerParams(
            dimension_semantics=("arbitrary",), vmem_limit_bytes=VMEM_LIMIT
        ),
    )(src, whole, positive, act, errors, w_dec)


def local(inputs, targets, w_enc, b_enc, w_dec, b_dec):
    src = lax.axis_index("layer").astype(jnp.int32)[None]
    whole = lax.all_gather(inputs[0], "latent", axis=0, tiled=True)
    positive, act, partial = forward(src, whole, w_enc[0], b_enc, w_dec[0], f32)
    spread = lax.psum_scatter(partial, "layer", scatter_dimension=0, tiled=True)
    recon = lax.psum_scatter(spread, "latent", scatter_dimension=1, tiled=True)
    error = recon[0] + b_dec[0] - targets[0].astype(f32)
    err_low = error.astype(bf16)[None]
    stacked = lax.all_gather(err_low, "latent", axis=1, tiled=True)
    errors = lax.all_gather(stacked, "layer", axis=0, tiled=True)
    grad_bdec = lax.psum(jnp.sum(error, axis=0), "latent")[None, :]
    grad_enc, grad_benc, grad_dec = backward(src, whole, positive, act, errors, w_dec[0])
    return (grad_enc[None], grad_benc, grad_dec[None], grad_bdec)


def solution(mesh):
    placed = (
        P("layer", "latent", None),
        P("layer", "latent", None),
        P("layer", None, "latent"),
        P("layer", "latent"),
        P("layer", None, "latent", None),
        P("layer", None),
    )
    return jax.shard_map(
        local,
        mesh=mesh,
        in_specs=placed,
        out_specs=(
            P("layer", None, "latent"),
            P("layer", "latent"),
            P("layer", None, "latent", None),
            P("layer", None),
        ),
        check_vma=False,
    )
```

time: 459 us -> 344 us (0.75)
  the two profiles are of different devices: /device:TPU:0 before, /device:TPU:16 now
where the time goes in v1:
time: 344 us; the launch traced here: 340 us
  waiting for transfers between devices  227 us (66%)
  Pallas kernels  64.5 us (19%)
  blocking collectives  31.8 us (9%)
  between operations  13.8 us (4%)
    reduce_scatter x1, waiting for transfers between devices, local(): spread = lax.psum_scatter(partial, 'layer', scatter_dimension=0, tiled=True)  71.1 us
    reduce_scatter x1, waiting for transfers between devices, local(): recon = lax.psum_scatter(spread, 'latent', scatter_dimension=1, tiled=True)  70.7 us
    pallas_call x1, Pallas kernels, backward(): pl.pallas_call(backward_kernel, grid_spec=pltpu.PrefetchScalarGridSpec(nu...  43.8 us
    all_gather x1, waiting for transfers between devices, local(): whole = lax.all_gather(inputs[0], 'latent', axis=0, tiled=True)  41.7 us
    all_gather x1, waiting for transfers between devices, local(): stacked = lax.all_gather(err_low, 'latent', axis=1, tiled=True)  39.5 us
    psum x1, blocking collectives, local(): grad_bdec = lax.psum(jnp.sum(error, axis=0), 'latent')[None, :]  31.8 us
    pallas_call x1, Pallas kernels, forward(): pl.pallas_call(forward_kernel, grid_spec=pltpu.PrefetchScalarGridSpec(num...  20.8 us
  transfers between devices with their start and end apart: 5, of which 5 were waited for; matrix products, arithmetic and copies ran while one was open for 0% of the time, Pallas kernels for 0%

profile of v1, /device:TPU:16, one launch (start us, length us, event | category | flops | bytes accessed | tf_op | source)
XLA Modules:
  0.0 340.4 jit_solution(3385928745613003196)
XLA Ops:
  7.2 0.0 all-gather.9.cloned.1.call-start
  7.2 0.7 all-gather.9.cloned.1.call-update
  7.9 0.0 reduce-scatter.3.cloned.1.call-start
  8.0 41.7 %all-gather.9.cloned.1.call-done = bf16[1,128,4096]{2,1,0:T(8,128)(2,1)} async-done(((bf16[1,16,4096]{2,1,0:T(8,128)(2,1)}), bf16[1,128,4096]{2,1,0:T(8,128)(2,1)}) %all-gather.9.cloned.1.call-update) | async-done | bytes 1048592 | tf_op jit(solution)/shard_map/all_gather | solution.py:171
  49.7 20.8 %shard_map.93 = (f32[128,1024]{1,0:T(8,128)}, bf16[128,1024]{1,0:T(8,128)(2,1)}, f32[4,128,4096]{2,1,0:T(8,128)}) custom-call(s32[1]{0:T(128)} %bitcast.src, bf16[128,4096]{1,0:T(8,128)(2,1)} %bitcast.21, bf16[4096,1024]{1,0:T(8,128)(2,1)} %bitcast.20, f32[1,1024]{1,0:T(1,128)} %b_enc.1, bf16[4,1024,4096]{2,1,0:T(8,128)(2,1)} %bitcast.18), custom_call_target="tpu_custom_call" | custom-call | tf_op jit(solution)/shard_map/pallas_call | solution.py:50
  70.5 0.0 copy-start
  70.5 0.0 copy-start.1
  70.5 0.0 reduce-scatter.3.cloned.1.call-update
  70.5 0.0 reduce-scatter.5.cloned.1.call-start
  70.5 71.1 %reduce-scatter.3.cloned.1.call-done = f32[1,128,4096]{2,1,0:T(8,128)} async-done(((f32[4,128,4096]{2,1,0:T(8,128)}), f32[1,128,4096]{2,1,0:T(8,128)}) %reduce-scatter.3.cloned.1.call-update) | async-done | bytes 2097168 | tf_op jit(solution)/shard_map/reduce_scatter | solution.py:173
  141.7 0.0 reduce-scatter.5.cloned.1.call-update
  141.7 0.0 all-gather.5.cloned.1.call-start
  141.7 70.7 %reduce-scatter.5.cloned.1.call-done = f32[1,16,4096]{2,1,0:T(8,128)} async-done(((f32[1,128,4096]{2,1,0:T(8,128)}), f32[1,16,4096]{2,1,0:T(8,128)}) %reduce-scatter.5.cloned.1.call-update) | async-done | bytes 262160 | tf_op jit(solution)/shard_map/reduce_scatter | solution.py:174
  212.4 0.0 copy-done
  212.4 0.0 copy-done.1
  212.4 1.6 fusion
  214.1 0.0 all-gather.5.cloned.1.call-update
  214.1 0.0 all-gather.7.cloned.1.call-start
  214.1 39.5 %all-gather.5.cloned.1.call-done = bf16[1,128,4096]{2,1,0:T(8,128)(2,1)} async-done(((bf16[1,16,4096]{2,1,0:T(8,128)(2,1)}), bf16[1,128,4096]{2,1,0:T(8,128)(2,1)}) %all-gather.5.cloned.1.call-update) | async-done | bytes 1048592 | tf_op jit(solution)/shard_map/all_gather | solution.py:177
  253.7 0.0 all-gather.7.cloned.1.call-update
  253.7 1.0 fusion.2
  254.7 31.8 %psum.7 = f32[1,4096]{1,0:T(1,128)} all-reduce(f32[1,4096]{1,0:T(1,128)S(1)} %bitcast.25), channel_id=1, replica_groups=mesh['layer'=4,'latent'=8] {'latent'}, use_global_device_ids=true, to_apply=%region_3.0 | all-reduce | flops 4096 | bytes 32768 | tf_op jit(solution)/shard_map/psum | solution.py:179
  286.5 3.5 %all-gather.7.cloned.1.call-done.errors = bf16[4,128,4096]{2,1,0:T(8,128)(2,1)} async-done(((bf16[1,128,4096]{2,1,0:T(8,128)(2,1)}), bf16[4,128,4096]{2,1,0:T(8,128)(2,1)}) %all-gather.7.cloned.1.call-update) | async-done | bytes 4194320 | tf_op jit(solution)/shard_map/all_gather | solution.py:178
  290.1 43.8 %shard_map.94 = (bf16[4096,1024]{1,0:T(8,128)(2,1)}, f32[1,1024]{1,0:T(1,128)}, bf16[4,1024,4096]{2,1,0:T(8,128)(2,1)}) custom-call(s32[1]{0:T(128)} %bitcast.src, bf16[128,4096]{1,0:T(8,128)(2,1)} %bitcast.22, f32[128,1024]{1,0:T(8,128)} %get-tuple-element.10.positive, bf16[128,1024]{1,0:T(8,128)(2,1)} %get-tuple-element.11.act, ...), custom_call_target="tpu_custom_call" | custom-call | tf_op jit(solution)/shard_map/pallas_call | solution.py:135
Async XLA Ops:
  7.2 42.5 %all-gather.9.cloned.1.call-start = ((), (), s32[]{:S(2)}) async-start(), calls=%async_computation.6 | async-start | bytes 1179648 | tf_op jit(solution)/shard_map/all_gather | solution.py:171
  7.9 133.8 %reduce-scatter.3.cloned.1.call-start = ((), (), s32[]{:S(2)}) async-start(), calls=%async_computation.2 | async-start | bytes 10485760 | tf_op jit(solution)/shard_map/reduce_scatter | solution.py:173
  70.5 142.0 %copy-start = (bf16[1,16,4096]{2,1,0:T(8,128)(2,1)S(1)}, bf16[1,16,4096]{2,1,0:T(8,128)(2,1)}, u32[]{:S(2)}) copy-start(bf16[1,16,4096]{2,1,0:T(8,128)(2,1)} %param.7) | copy-start | bytes 393220
  70.5 142.0 %copy-start.1 = (f32[1,4096]{1,0:T(1,128)S(1)}, f32[1,4096]{1,0:T(1,128)}, u32[]{:S(2)}) copy-start(f32[1,4096]{1,0:T(1,128)} %param.11) | copy-start | bytes 49156
  70.5 141.9 %reduce-scatter.5.cloned.1.call-start = ((), (), s32[]{:S(2)}) async-start(), calls=%async_computation.3 | async-start | bytes 2359296 | tf_op jit(solution)/shard_map/reduce_scatter | solution.py:174
  141.7 112.0 %all-gather.5.cloned.1.call-start = ((), (), s32[]{:S(2)}) async-start(), calls=%async_computation.4 | async-start | bytes 1179648 | tf_op jit(solution)/shard_map/all_gather | solution.py:177
  214.1 76.0 %all-gather.7.cloned.1.call-start = ((), (), s32[]{:S(2)}) async-start(), calls=%async_computation.5 | async-start | bytes 5242880 | tf_op jit(solution)/shard_map/all_gather | solution.py:178
Sparse Core Ops, SparseCore 0:
  10.1 39.5 all-gather.8
  70.6 70.9 reduce-scatter.2
  145.2 67.1 reduce-scatter.4
  215.0 38.6 all-gather.4
  255.1 34.9 all-gather.6

commit v2 on v1

--- a/solution.py
+++ b/solution.py
@@ -166,17 +166,316 @@
     )(src, whole, positive, act, errors, w_dec)
 
 
+MESH = pl.DeviceIdType.MESH
+
+
+def place():
+    layer, latent = lax.axis_index("layer"), lax.axis_index("latent")
+    return layer // 2, lax.rem(layer, 2), latent // 2, lax.rem(latent, 2)
+
+
+def remote(src, dst, send, recv, target):
+    return pltpu.make_async_remote_copy(
+        src_ref=src, dst_ref=dst, send_sem=send, recv_sem=recv, device_id=target, device_id_type=MESH
+    )
+
+
+def greet(partners):
+    barrier = pltpu.get_barrier_semaphore()
+    for partner in partners:
+        pl.semaphore_signal(barrier, inc=1, device_id=partner, device_id_type=MESH)
+    pl.semaphore_wait(barrier, len(partners))
+
+
+def gather_kernel(rows, own, whole, send_z, recv_z, send_x, recv_x):
+    y, c, z, x = place()
+    layer = 2 * y + c
+    mine = 2 * z + x
+    beside = (layer, 2 * z + 1 - x)
+    along = [(layer, 2 * lax.rem(z + d, rows) + x) for d in range(rows)]
+    greet([beside] + along[1:])
+    sent = []
+    order = sorted(range(1, rows), key=lambda d: abs(2 * d - rows))
+    for d in order:
+        copy = remote(own, whole.at[mine], send_z.at[d], recv_z.at[d], along[d])
+        copy.start()
+        sent.append(copy)
+    first = remote(own, whole.at[mine], send_x.at[0], recv_x.at[0], beside)
+    first.start()
+    whole[mine] = own[...]
+    across = [first]
+    for d in range(1, rows):
+        start = 2 * lax.rem(z + rows - d, rows) + x
+        remote(own, whole.at[start], send_z.at[d], recv_z.at[d], along[d]).wait_recv()
+        copy = remote(whole.at[start], whole.at[start], send_x.at[d], recv_x.at[d], beside)
+        copy.start()
+        across.append(copy)
+    for copy in sent:
+        copy.wait_send()
+    for copy in across:
+        copy.wait()
+
+
+def gather(block, peers):
+    tokens, features = block.shape
+    rows = peers // 2
+    dma = pltpu.SemaphoreType.DMA((rows,))
+    return pl.pallas_call(
+        functools.partial(gather_kernel, rows),
+        out_shape=jax.ShapeDtypeStruct((peers, tokens, features), bf16),
+        in_specs=[pl.BlockSpec(memory_space=pltpu.VMEM)],
+        out_specs=pl.BlockSpec(memory_space=pltpu.VMEM),
+        scratch_shapes=[dma] * 4,
+        compiler_params=pltpu.CompilerParams(collective_id=0, has_side_effects=True),
+    )(block).reshape(peers * tokens, features)
+
+
+def exchange_kernel(
+    rows, part, targets, b_dec, errors, grad_bdec,
+    core_in, out_x, in_x, out_z, in_z, own, out_y, in_y, biases,
+    send_c, recv_c, send_x, recv_x, send_z, recv_z, send_y, recv_y,
+    send_ez, recv_ez, send_ex, recv_ex, send_ec, recv_ec, send_b, recv_b,
+):
+    y, c, z, x = place()
+    layer = 2 * y + c
+    mine = 2 * z + x
+    peers = 2 * rows
+    core = (2 * y + 1 - c, mine)
+    beside = (layer, 2 * z + 1 - x)
+    across = (2 * (1 - y) + c, mine)
+    along = [(layer, 2 * lax.rem(z + d, rows) + x) for d in range(rows)]
+    everyone = [(layer, lax.rem(mine + o, peers)) for o in range(peers)]
+    greet([core, across] + everyone[1:])
+    bottom, top = y == 0, y == 1
+
+    def only(k, body):
+        if k == 1:
+            body()
+        else:
+            pl.when(bottom)(body)
+
+    def pair(d):
+        return pl.ds(2 * lax.rem(z + d, rows), 2)
+
+    def core_copy(k, d):
+        return remote(
+            part.at[1 - c + 2 * k, pair(d)], core_in.at[k, pair(d)], send_c.at[k, d], recv_c.at[k, d], core
+        )
+
+    def x_copy(k, d):
+        return remote(out_x.at[k, d], in_x.at[k, d], send_x.at[k, d], recv_x.at[k, d], beside)
+
+    def z_copy(k, d):
+        return remote(out_z.at[k, d], in_z.at[k, d], send_z.at[k, d], recv_z.at[k, d], along[d])
+
+    def both(k, at):
+        return part[c + 2 * k, at].astype(f32) + core_in[k, at].astype(f32)
+
+    def first(k, d):
+        def body():
+            core_copy(k, d).wait_recv()
+            at = 2 * lax.rem(z + d, rows) + 1 - x
+            out_x[k, d] = both(k, at).astype(bf16)
+            x_copy(k, d).start()
+
+        only(k, body)
+
+    def second(k, d):
+        def body():
+            x_copy(k, d).wait_recv()
+            at = 2 * lax.rem(z + d, rows) + x
+            value = both(k, at) + in_x[k, d].astype(f32)
+            if d == 0:
+                own[k] = value
+            else:
+                out_z[k, d] = value.astype(bf16)
+                z_copy(k, d).start()
+
+        only(k, body)
+
+    def collect(k):
+        value = own[k]
+        for d in range(1, rows):
+            z_copy(k, d).wait_recv()
+            value = value + in_z[k, d].astype(f32)
+        return value
+
+    def bias_copy(o):
+        return remote(biases.at[mine], biases.at[mine], send_b.at[o], recv_b.at[o], everyone[o])
+
+    def settle(value, k):
+        error = value + b_dec[...] - targets[...].astype(f32)
+        errors[c + 2 * k, mine] = error.astype(bf16)
+        total = jnp.sum(error, axis=0, keepdims=True)
+        width = total.shape[1] // 8
+        for i in range(8):
+            biases[mine, i : i + 1, :] = total[:, i * width : (i + 1) * width]
+
+    up = remote(out_y, in_y, send_y.at[0], recv_y.at[0], across)
+    high = errors.at[c + 2, mine]
+    down = remote(high, high, send_y.at[1], recv_y.at[1], across)
+
+    def spread_z(k, d):
+        ref = errors.at[c + 2 * k, mine]
+        return remote(ref, ref, send_ez.at[k, d], recv_ez.at[k, d], along[d])
+
+    def spread_x(k, d):
+        ref = errors.at[c + 2 * k, 2 * lax.rem(z + rows - d, rows) + x]
+        return remote(ref, ref, send_ex.at[k, d], recv_ex.at[k, d], beside)
+
+    def spread_c(k, d, side):
+        ref = errors.at[side + 2 * k, pl.ds(2 * lax.rem(z + rows - d, rows), 2)]
+        return remote(ref, ref, send_ec.at[k, d], recv_ec.at[k, d], core)
+
+    def launch(k):
+        for d in list(range(rows // 2, 0, -1)) + list(range(rows // 2 + 1, rows)):
+            spread_z(k, d).start()
+        spread_x(k, 0).start()
+
+    units = [(k, d) for k in (1, 0) for d in list(range(1, rows)) + [0]]
+    for k, d in units:
+        only(k, core_copy(k, d).start)
+    lag = 2
+    for i in range(len(units) + lag):
+        if i < len(units):
+            first(*units[i])
+        if i >= lag:
+            second(*units[i - lag])
+        if i == len(units) - 1:
+
+            @pl.when(bottom)
+            def _():
+                out_y[...] = collect(1).astype(bf16)
+                up.start()
+
+            @pl.when(top)
+            def _():
+                value = collect(1)
+                up.wait_recv()
+                settle(value + in_y[...].astype(f32), 1)
+                down.start()
+                launch(1)
+
+    @pl.when(bottom)
+    def _():
+        settle(collect(0), 0)
+        launch(0)
+        down.wait_recv()
+        launch(1)
+
+    for o in range(1, peers):
+        bias_copy(o).start()
+
+    for k in (0, 1):
+
+        def relay(k=k):
+            for d in range(1, rows):
+                spread_z(k, d).wait_recv()
+                spread_x(k, d).start()
+
+        only(k, relay)
+
+    forwards = {1: jnp.logical_or(bottom, c == 1), 0: jnp.logical_and(bottom, c == 1)}
+    receives = {1: jnp.logical_or(bottom, c == 0), 0: jnp.logical_and(bottom, c == 0)}
+    for k in (0, 1):
+
+        def finish(k=k):
+            for d in range(rows):
+                spread_x(k, d).wait_recv()
+
+                @pl.when(forwards[k])
+                def _():
+                    spread_c(k, d, c).start()
+
+        only(k, finish)
+
+    for o in range(1, peers):
+        bias_copy(o).wait()
+    total = biases[0]
+    for i in range(1, peers):
+        total = total + biases[i]
+    grad_bdec[...] = total
+
+    for k in (0, 1):
+
+        @pl.when(receives[k])
+        def _():
+            for d in range(rows):
+                spread_c(k, d, 1 - c).wait_recv()
+
+        @pl.when(forwards[k])
+        def _():
+            for d in range(rows):
+                spread_c(k, d, c).wait_send()
+
+        def drain(k=k):
+            for d in range(rows):
+                core_copy(k, d).wait_send()
+                x_copy(k, d).wait_send()
+                spread_x(k, d).wait_send()
+                if d:
+                    z_copy(k, d).wait_send()
+                    spread_z(k, d).wait_send()
+
+        only(k, drain)
+
+    pl.when(bottom)(up.wait_send)
+    pl.when(top)(down.wait_send)
+
+
+def exchange(partial, targets, b_dec, peers):
+    depth, tokens, features = partial.shape
+    rows = peers // 2
+    chunk = tokens // peers
+    slots = pltpu.VMEM((2, rows, chunk, features), bf16)
+    dma = pltpu.SemaphoreType.DMA((2, rows))
+    flat = pltpu.SemaphoreType.DMA((peers,))
+    errors, grad_bdec = pl.pallas_call(
+        functools.partial(exchange_kernel, rows),
+        out_shape=[
+            jax.ShapeDtypeStruct((depth, peers, chunk, features), bf16),
+            jax.ShapeDtypeStruct((8, features // 8), f32),
+        ],
+        in_specs=[pl.BlockSpec(memory_space=pltpu.VMEM)] * 3,
+        out_specs=[pl.BlockSpec(memory_space=pltpu.VMEM)] * 2,
+        scratch_shapes=[
+            pltpu.VMEM((2, peers, chunk, features), bf16),
+            slots, slots, slots, slots,
+            pltpu.VMEM((2, chunk, features), f32),
+            pltpu.VMEM((chunk, features), bf16),
+            pltpu.VMEM((chunk, features), bf16),
+            pltpu.VMEM((peers, 8, features // 8), f32),
+        ] + [dma] * 6 + [pltpu.SemaphoreType.DMA((2,))] * 2 + [dma] * 6 + [flat] * 2,
+        compiler_params=pltpu.CompilerParams(
+            collective_id=1, has_side_effects=True, vmem_limit_bytes=VMEM_LIMIT
+        ),
+    )(partial.reshape(depth, peers, chunk, features), targets, b_dec)
+    return errors.reshape(depth, tokens, features), grad_bdec.reshape(1, features)
+
+
+def paired(depth, peers, chunk, features):
+    layers = lax.axis_size("layer")
+    return layers == depth == 4 and peers % 2 == 0 and chunk % 16 == 0 and features % 1024 == 0
+
+
 def local(inputs, targets, w_enc, b_enc, w_dec, b_dec):
     src = lax.axis_index("layer").astype(jnp.int32)[None]
-    whole = lax.all_gather(inputs[0], "latent", axis=0, tiled=True)
-    positive, act, partial = forward(src, whole, w_enc[0], b_enc, w_dec[0], f32)
-    spread = lax.psum_scatter(partial, "layer", scatter_dimension=0, tiled=True)
-    recon = lax.psum_scatter(spread, "latent", scatter_dimension=1, tiled=True)
-    error = recon[0] + b_dec[0] - targets[0].astype(f32)
-    err_low = error.astype(bf16)[None]
-    stacked = lax.all_gather(err_low, "latent", axis=1, tiled=True)
-    errors = lax.all_gather(stacked, "layer", axis=0, tiled=True)
-    grad_bdec = lax.psum(jnp.sum(error, axis=0), "latent")[None, :]
+    peers = lax.axis_size("latent")
+    direct = paired(w_dec.shape[1], peers, inputs.shape[1], inputs.shape[2])
+    if direct:
+        whole = gather(inputs[0], peers)
+        positive, act, partial = forward(src, whole, w_enc[0], b_enc, w_dec[0], bf16)
+        errors, grad_bdec = exchange(partial, targets[0], b_dec, peers)
+    else:
+        whole = lax.all_gather(inputs[0], "latent", axis=0, tiled=True)
+        positive, act, partial = forward(src, whole, w_enc[0], b_enc, w_dec[0], f32)
+        spread = lax.psum_scatter(partial, "layer", scatter_dimension=0, tiled=True)
+        recon = lax.psum_scatter(spread, "latent", scatter_dimension=1, tiled=True)
+        error = recon[0] + b_dec[0] - targets[0].astype(f32)
+        err_low = error.astype(bf16)[None]
+        stacked = lax.all_gather(err_low, "latent", axis=1, tiled=True)
+        errors = lax.all_gather(stacked, "layer", axis=0, tiled=True)
+        grad_bdec = lax.psum(jnp.sum(error, axis=0), "latent")[None, :]
     grad_enc, grad_benc, grad_dec = backward(src, whole, positive, act, errors, w_dec[0])
     return (grad_enc[None], grad_benc, grad_dec[None], grad_bdec)
 

time: 344 us -> 165 us (0.48); the launches traced: 340 us -> 165 us
  waiting for transfers between devices: 227 us -> 0 us
  Pallas kernels: 64.5 us -> 163 us
  blocking collectives: 31.8 us -> 0 us
  between operations: 13.8 us -> 0.65 us
    reduce_scatter x2 -> x0, waiting for transfers between devices: 142 us -> none  [the longest x1 71.1 us: local(): spread = lax.psum_scatter(partial, 'layer', scatter_dimension=0, tiled=True)]
    pallas_call x0 -> x2, Pallas kernels: none -> 99.9 us  [the longest x1 73.3 us: exchange(): pl.pallas_call(functools.partial(exchange_kernel, rows), out_shape=[jax.S...]
    all_gather x3 -> x0, waiting for transfers between devices: 84.8 us -> none  [the longest x1 41.7 us: local(): whole = lax.all_gather(inputs[0], 'latent', axis=0, tiled=True)]
    psum x1 -> x0, blocking collectives: 31.8 us -> none  [local(): grad_bdec = lax.psum(jnp.sum(error, axis=0), 'latent')[None, :]]
  transfers between devices with their start and end apart: 5 -> 0, of which waited for: 5 -> 0; matrix products, arithmetic and copies ran while one was open for 0% -> 0% of each run, Pallas kernels for 0% -> 0%
where the time goes in v2:
time: 165 us
  Pallas kernels  163 us (99%)
    pallas_call x1, Pallas kernels, exchange(): pl.pallas_call(functools.partial(exchange_kernel, rows), out_shape=[jax.S...  73.3 us
    pallas_call x1, Pallas kernels, backward(): pl.pallas_call(backward_kernel, grid_spec=pltpu.PrefetchScalarGridSpec(nu...  43.8 us
    pallas_call x1, Pallas kernels, gather(): pl.pallas_call(functools.partial(gather_kernel, rows), out_shape=jax.Shap...  26.6 us
    pallas_call x1, Pallas kernels, forward(): pl.pallas_call(forward_kernel, grid_spec=pltpu.PrefetchScalarGridSpec(num...  19.3 us

profile of v2, /device:TPU:16, one launch (start us, length us, event | category | flops | bytes accessed | tf_op | source)
XLA Modules:
  0.0 164.9 jit_solution(17768465502507461388)
XLA Ops:
  0.6 26.6 %shard_map.93 = bf16[8,16,4096]{2,1,0:T(8,128)(2,1)} custom-call(bf16[16,4096]{1,0:T(8,128)(2,1)} %bitcast.20), custom_call_target="tpu_custom_call" | custom-call | tf_op jit(solution)/shard_map/pallas_call | solution.py:223
  27.2 19.3 %shard_map.94 = (f32[128,1024]{1,0:T(8,128)}, bf16[128,1024]{1,0:T(8,128)(2,1)}, bf16[4,128,4096]{2,1,0:T(8,128)(2,1)}) custom-call(s32[1]{0:T(128)} %bitcast.src, bf16[128,4096]{1,0:T(8,128)(2,1)} %bitcast.15, bf16[4096,1024]{1,0:T(8,128)(2,1)} %bitcast.17, f32[1,1024]{1,0:T(1,128)} %b_enc.1, bf16[4,1024,4096]{2,1,0:T(8,128)(2,1)} %bitcast.13), custom_call_target="tpu_custom_call" | custom-call | tf_op jit(solution)/shard_map/pallas_call | solution.py:50
  46.5 73.3 %shard_map.95 = (bf16[4,8,16,4096]{3,2,1,0:T(8,128)(2,1)}, f32[8,512]{1,0:T(8,128)}) custom-call(bf16[4,8,16,4096]{3,2,1,0:T(8,128)(2,1)} %bitcast.18, bf16[16,4096]{1,0:T(8,128)(2,1)} %bitcast.21, f32[1,4096]{1,0:T(1,128)} %b_dec.1), custom_call_target="tpu_custom_call" | custom-call | tf_op jit(solution)/shard_map/pallas_call | solution.py:433
  119.8 1.3 copy.10
  121.2 43.8 %shard_map.96 = (bf16[4096,1024]{1,0:T(8,128)(2,1)}, f32[1,1024]{1,0:T(1,128)}, bf16[4,1024,4096]{2,1,0:T(8,128)(2,1)}) custom-call(s32[1]{0:T(128)} %bitcast.src, bf16[128,4096]{1,0:T(8,128)(2,1)} %bitcast.16, f32[128,1024]{1,0:T(8,128)} %get-tuple-element.12.positive, bf16[128,1024]{1,0:T(8,128)(2,1)} %get-tuple-element.13.act, ...), custom_call_target="tpu_custom_call" | custom-call | tf_op jit(solution)/shard_map/pallas_call | solution.py:135

commit v3 on v2

--- a/solution.py
+++ b/solution.py
@@ -14,7 +14,11 @@
 VMEM_LIMIT = 60 * 1024 * 1024
 
 
-def forward_kernel(src, whole, w_enc, b_enc, w_dec, positive, act, partial, total):
+def forward_kernel(src, *refs):
+    forward_body(src[0], *refs)
+
+
+def forward_body(layer, whole, w_enc, b_enc, w_dec, positive, act, partial, total):
     step = pl.program_id(0)
     depth = w_dec.shape[0]
     features = w_dec.shape[2]
@@ -30,7 +34,7 @@
     act[...] = (pos * pos).astype(bf16)
     for t in range(depth):
 
-        @pl.when(t >= src[0])
+        @pl.when(t >= layer)
         def _():
             for c in range(0, features, cols):
                 total[t, :, c : c + cols] += jnp.dot(
@@ -131,7 +135,7 @@
 def backward(src, whole, positive, act, errors, w_dec):
     tokens, features = whole.shape
     depth, latents, _ = w_dec.shape
-    block = min(latents, 128)
+    block = min(latents, 256)
     return pl.pallas_call(
         backward_kernel,
         grid_spec=pltpu.PrefetchScalarGridSpec(
@@ -216,18 +220,62 @@
         copy.wait()
 
 
-def gather(block, peers):
-    tokens, features = block.shape
+def joined_kernel(
+    rows, own, w_enc, b_enc, w_dec, positive, act, partial, everything,
+    total, landing, send_z, recv_z, send_x, recv_x,
+):
+    @pl.when(pl.program_id(0) == 0)
+    def _():
+        gather_kernel(rows, own, landing, send_z, recv_z, send_x, recv_x)
+        for i in range(2 * rows):
+            chunk = own.shape[0]
+            everything[i * chunk : (i + 1) * chunk, :] = landing[i]
+
+    forward_body(
+        lax.axis_index("layer"), everything, w_enc, b_enc, w_dec, positive, act, partial, total
+    )
+
+
+def joined(own, w_enc, b_enc, w_dec, peers):
+    chunk, features = own.shape
+    tokens = chunk * peers
+    depth, latents, _ = w_dec.shape
+    block = min(latents, 256)
     rows = peers // 2
     dma = pltpu.SemaphoreType.DMA((rows,))
     return pl.pallas_call(
-        functools.partial(gather_kernel, rows),
-        out_shape=jax.ShapeDtypeStruct((peers, tokens, features), bf16),
-        in_specs=[pl.BlockSpec(memory_space=pltpu.VMEM)],
-        out_specs=pl.BlockSpec(memory_space=pltpu.VMEM),
-        scratch_shapes=[dma] * 4,
-        compiler_params=pltpu.CompilerParams(collective_id=0, has_side_effects=True),
-    )(block).reshape(peers * tokens, features)
+        functools.partial(joined_kernel, rows),
+        grid_spec=pltpu.PrefetchScalarGridSpec(
+            num_scalar_prefetch=0,
+            grid=(latents // block,),
+            in_specs=[
+                pl.BlockSpec((chunk, features), lambda i: (0, 0), pipeline_mode=pl.Buffered(1)),
+                pl.BlockSpec((features, block), lambda i: (0, i)),
+                pl.BlockSpec((1, block), lambda i: (0, i)),
+                pl.BlockSpec((depth, block, features), lambda i: (0, i, 0)),
+            ],
+            out_specs=[
+                pl.BlockSpec((tokens, block), lambda i: (0, i)),
+                pl.BlockSpec((tokens, block), lambda i: (0, i)),
+                pl.BlockSpec((depth, tokens, features), lambda i: (0, 0, 0), pipeline_mode=pl.Buffered(1)),
+                pl.BlockSpec((tokens, features), lambda i: (0, 0), pipeline_mode=pl.Buffered(1)),
+            ],
+            scratch_shapes=[
+                pltpu.VMEM((depth, tokens, features), f32),
+                pltpu.VMEM((peers, chunk, features), bf16),
+            ] + [dma] * 4,
+        ),
+        out_shape=[
+            jax.ShapeDtypeStruct((tokens, latents), f32),
+            jax.ShapeDtypeStruct((tokens, latents), bf16),
+            jax.ShapeDtypeStruct((depth, tokens, features), bf16),
+            jax.ShapeDtypeStruct((tokens, features), bf16),
+        ],
+        compiler_params=pltpu.CompilerParams(
+            dimension_semantics=("arbitrary",), vmem_limit_bytes=VMEM_LIMIT,
+            collective_id=0, has_side_effects=True,
+        ),
+    )(own, w_enc, b_enc, w_dec)
 
 
 def exchange_kernel(
@@ -394,7 +442,9 @@
     total = biases[0]
     for i in range(1, peers):
         total = total + biases[i]
-    grad_bdec[...] = total
+    width = total.shape[1]
+    for i in range(8):
+        grad_bdec[:, i * width : (i + 1) * width] = total[i : i + 1, :]
 
     for k in (0, 1):
 
@@ -434,7 +484,7 @@
         functools.partial(exchange_kernel, rows),
         out_shape=[
             jax.ShapeDtypeStruct((depth, peers, chunk, features), bf16),
-            jax.ShapeDtypeStruct((8, features // 8), f32),
+            jax.ShapeDtypeStruct((1, features), f32),
         ],
         in_specs=[pl.BlockSpec(memory_space=pltpu.VMEM)] * 3,
         out_specs=[pl.BlockSpec(memory_space=pltpu.VMEM)] * 2,
@@ -450,7 +500,7 @@
             collective_id=1, has_side_effects=True, vmem_limit_bytes=VMEM_LIMIT
         ),
     )(partial.reshape(depth, peers, chunk, features), targets, b_dec)
-    return errors.reshape(depth, tokens, features), grad_bdec.reshape(1, features)
+    return errors.reshape(depth, tokens, features), grad_bdec
 
 
 def paired(depth, peers, chunk, features):
@@ -463,8 +513,7 @@
     peers = lax.axis_size("latent")
     direct = paired(w_dec.shape[1], peers, inputs.shape[1], inputs.shape[2])
     if direct:
-        whole = gather(inputs[0], peers)
-        positive, act, partial = forward(src, whole, w_enc[0], b_enc, w_dec[0], bf16)
+        positive, act, partial, whole = joined(inputs[0], w_enc[0], b_enc, w_dec[0], peers)
         errors, grad_bdec = exchange(partial, targets[0], b_dec, peers)
     else:
         whole = lax.all_gather(inputs[0], "latent", axis=0, tiled=True)

time: 165 us -> 164 us (level)
    pallas_call x2 -> x1, Pallas kernels: 45.9 us -> 44.5 us  [joined(): pl.pallas_call(functools.partial(joined_kernel, rows), grid_spec=pltpu.Pr...]
where the time goes in v3:
time: 164 us
  Pallas kernels  162 us (99%)
    pallas_call x1, Pallas kernels, exchange(): pl.pallas_call(functools.partial(exchange_kernel, rows), out_shape=[jax.S...  73.3 us
    pallas_call x1, Pallas kernels, joined(): pl.pallas_call(functools.partial(joined_kernel, rows), grid_spec=pltpu.Pr...  44.5 us
    pallas_call x1, Pallas kernels, backward(): pl.pallas_call(backward_kernel, grid_spec=pltpu.PrefetchScalarGridSpec(nu...  44.5 us

profile of v3, /device:TPU:16, one launch (start us, length us, event | category | flops | bytes accessed | tf_op | source)
XLA Modules:
  0.0 163.5 jit_solution(2080453302618628314)
XLA Ops:
  0.6 44.5 %shard_map.93 = (f32[128,1024]{1,0:T(8,128)}, bf16[128,1024]{1,0:T(8,128)(2,1)}, bf16[4,128,4096]{2,1,0:T(8,128)(2,1)}, bf16[128,4096]{1,0:T(8,128)(2,1)}) custom-call(bf16[16,4096]{1,0:T(8,128)(2,1)} %bitcast.14, bf16[4096,1024]{1,0:T(8,128)(2,1)} %bitcast.11, f32[1,1024]{1,0:T(1,128)} %b_enc.1, bf16[4,1024,4096]{2,1,0:T(8,128)(2,1)} %bitcast.9), custom_call_target="tpu_custom_call" | custom-call | tf_op jit(solution)/shard_map/pallas_call | solution.py:246
  45.1 73.3 %shard_map.94 = (bf16[4,8,16,4096]{3,2,1,0:T(8,128)(2,1)}, f32[1,4096]{1,0:T(1,128)}) custom-call(bf16[4,8,16,4096]{3,2,1,0:T(8,128)(2,1)} %bitcast.12, bf16[16,4096]{1,0:T(8,128)(2,1)} %bitcast.15, f32[1,4096]{1,0:T(1,128)} %b_dec.1), custom_call_target="tpu_custom_call" | custom-call | tf_op jit(solution)/shard_map/pallas_call | solution.py:483
  118.5 0.0 copy-start
  118.5 44.5 %shard_map.95 = (bf16[4096,1024]{1,0:T(8,128)(2,1)}, f32[1,1024]{1,0:T(1,128)}, bf16[4,1024,4096]{2,1,0:T(8,128)(2,1)}) custom-call(s32[1]{0:T(128)} %bitcast.src, bf16[128,4096]{1,0:T(8,128)(2,1)} %get-tuple-element.13.whole, f32[128,1024]{1,0:T(8,128)} %get-tuple-element.14.positive, bf16[128,1024]{1,0:T(8,128)(2,1)} %get-tuple-element.15.act, ...), custom_call_target="tpu_custom_call" | custom-call | tf_op jit(solution)/shard_map/pallas_call | solution.py:139
  162.9 0.0 copy-done
  162.9 0.6 copy.11
Async XLA Ops:
  118.5 44.5 %copy-start = (f32[1,4096]{1,0:T(1,128)S(1)}, f32[1,4096]{1,0:T(1,128)}, u32[]{:S(2)}) copy-start(f32[1,4096]{1,0:T(1,128)} %get-tuple-element.29) | copy-start | bytes 49156

commit v4 on v3

--- a/solution.py
+++ b/solution.py
@@ -24,27 +24,40 @@
     features = w_dec.shape[2]
     cols = min(features, 1024)
 
-    @pl.when(step == 0)
-    def _():
-        total[...] = jnp.zeros_like(total)
-
+    last = pl.num_programs(0) - 1
     pre = jnp.dot(whole[...], w_enc[...], preferred_element_type=f32) + b_enc[...]
     pos = jnp.maximum(pre, 0.0)
     positive[...] = pos
     act[...] = (pos * pos).astype(bf16)
+
+    def term(t, c):
+        return jnp.dot(act[...], w_dec[t, :, c : c + cols], preferred_element_type=f32)
+
     for t in range(depth):
-
-        @pl.when(t >= layer)
+        used = t >= layer
+
+        @pl.when(used & (step == 0))
         def _():
             for c in range(0, features, cols):
-                total[t, :, c : c + cols] += jnp.dot(
-                    act[...], w_dec[t, :, c : c + cols], preferred_element_type=f32
-                )
-
-    @pl.when(step == pl.num_programs(0) - 1)
-    def _():
-        for t in range(depth):
+                total[t, :, c : c + cols] = term(t, c)
+
+        @pl.when(used & (step > 0) & (step < last))
+        def _():
+            for c in range(0, features, cols):
+                total[t, :, c : c + cols] += term(t, c)
+
+        @pl.when(used & (step > 0) & (step == last))
+        def _():
+            for c in range(0, features, cols):
+                partial[t, :, c : c + cols] = (total[t, :, c : c + cols] + term(t, c)).astype(partial.dtype)
+
+        @pl.when(used & (step == 0) & (step == last))
+        def _():
             partial[t] = total[t].astype(partial.dtype)
+
+        @pl.when((t < layer) & (step == last))
+        def _():
+            partial[t] = jnp.zeros_like(partial[t])
 
 
 def forward(src, whole, w_enc, b_enc, w_dec, out_dtype):

time: 164 us -> 163 us (level)
  no operation moved by 1% of the time
where the time goes in v4:
time: 163 us
  Pallas kernels  161 us (99%)
    pallas_call x1, Pallas kernels, exchange(): pl.pallas_call(functools.partial(exchange_kernel, rows), out_shape=[jax.S...  73.3 us
    pallas_call x1, Pallas kernels, backward(): pl.pallas_call(backward_kernel, grid_spec=pltpu.PrefetchScalarGridSpec(nu...  44.5 us
    pallas_call x1, Pallas kernels, joined(): pl.pallas_call(functools.partial(joined_kernel, rows), grid_spec=pltpu.Pr...  43.5 us

profile of v4, /device:TPU:16, one launch (start us, length us, event | category | flops | bytes accessed | tf_op | source)
XLA Modules:
  0.0 162.6 jit_solution(11127809076461502842)
XLA Ops:
  0.6 43.5 %shard_map.93 = (f32[128,1024]{1,0:T(8,128)}, bf16[128,1024]{1,0:T(8,128)(2,1)}, bf16[4,128,4096]{2,1,0:T(8,128)(2,1)}, bf16[128,4096]{1,0:T(8,128)(2,1)}) custom-call(bf16[16,4096]{1,0:T(8,128)(2,1)} %bitcast.14, bf16[4096,1024]{1,0:T(8,128)(2,1)} %bitcast.11, f32[1,1024]{1,0:T(1,128)} %b_enc.1, bf16[4,1024,4096]{2,1,0:T(8,128)(2,1)} %bitcast.9), custom_call_target="tpu_custom_call" | custom-call | tf_op jit(solution)/shard_map/pallas_call | solution.py:259
  44.2 73.3 %shard_map.94 = (bf16[4,8,16,4096]{3,2,1,0:T(8,128)(2,1)}, f32[1,4096]{1,0:T(1,128)}) custom-call(bf16[4,8,16,4096]{3,2,1,0:T(8,128)(2,1)} %bitcast.12, bf16[16,4096]{1,0:T(8,128)(2,1)} %bitcast.15, f32[1,4096]{1,0:T(1,128)} %b_dec.1), custom_call_target="tpu_custom_call" | custom-call | tf_op jit(solution)/shard_map/pallas_call | solution.py:496
  117.5 0.0 copy-start
  117.5 44.5 %shard_map.95 = (bf16[4096,1024]{1,0:T(8,128)(2,1)}, f32[1,1024]{1,0:T(1,128)}, bf16[4,1024,4096]{2,1,0:T(8,128)(2,1)}) custom-call(s32[1]{0:T(128)} %bitcast.src, bf16[128,4096]{1,0:T(8,128)(2,1)} %get-tuple-element.13.whole, f32[128,1024]{1,0:T(8,128)} %get-tuple-element.14.positive, bf16[128,1024]{1,0:T(8,128)(2,1)} %get-tuple-element.15.act, ...), custom_call_target="tpu_custom_call" | custom-call | tf_op jit(solution)/shard_map/pallas_call | solution.py:152
  162.0 0.0 copy-done
  162.0 0.6 copy.11
Async XLA Ops:
  117.5 44.5 %copy-start = (f32[1,4096]{1,0:T(1,128)S(1)}, f32[1,4096]{1,0:T(1,128)}, u32[]{:S(2)}) copy-start(f32[1,4096]{1,0:T(1,128)} %get-tuple-element.29) | copy-start | bytes 49156
